TPU v7x, 128 devices: a whole 4x4x4 slice. The times are simulated.
128 devices in a mesh: sta: 16 (over y_hi, z, core), tpl: 8 (over y_lo, x).
Axes of the slice: x: 4, y: 4 (y_hi: 2, y_lo: 2; y = y_hi * 2 + y_lo), z: 4, core: 2. Of those that a mesh axis runs over, the one named last changes fastest.
Arguments:
- records: bfloat16 [16, 3, 32768], P('sta', None, 'tpl'), may hold values from -36 to 36
- templates: bfloat16 [256, 16, 3, 600], P('tpl', 'sta'), may hold values from -12 to 12
- moveouts: int32 [256, 16], P('tpl', 'sta'), may hold values from 0 to 63
Outputs:
- detection_stack: float32 [256, 16384], P('sta', 'tpl')
Inputs may be any that keep to these rules, and one draw needn't show every extreme that they name: `moveouts`: lag offset at which station s joins the sum for template k.
All inputs are finite; a program needn't handle non-finite values.
Results may differ from a plain program's by a relative error of at most 0.0029.
Values may be sent and summed in bfloat16 or wider, within the bound.
A program may use at most 128 MiB of HBM per device.

v0:
```python
import functools

import jax
import jax.numpy as jnp
from jax import lax
from jax.experimental import pallas as pl
from jax.experimental.pallas import tpu as pltpu
from jax.sharding import PartitionSpec as P

MESH = pl.DeviceIdType.MESH
F32, BF16 = jnp.float32, jnp.bfloat16
COMP = 3
LENGTH = 600
SEG = 4096
HALO = 768
WIDE = SEG + HALO
TAPS = 768
SPREAD = 256
SHARE = 32
HALF = 16
SUB = 8
ROWS = 256


def gather_kernel(rec_ref, tmpl_ref, mov_ref, all_ref, filt_ref, pick_ref, pad, send, recv, home):
    s, t = lax.axis_index("sta"), lax.axis_index("tpl")
    h = lax.rem(s, 2)
    barrier = pltpu.get_barrier_semaphore()
    for i in range(1, 8):
        pl.semaphore_signal(barrier, inc=1, device_id=(s, lax.rem(t + i, 8)), device_id_type=MESH)

    pad[...] = jnp.zeros_like(pad)
    moves = jnp.broadcast_to(mov_ref[...], (SHARE, TAPS))

    def filters(c):
        shape = tmpl_ref[:, c, :].astype(F32)
        factor = lax.rsqrt(jnp.sum(shape * shape, axis=1, keepdims=True) / LENGTH + 1e-05)
        pad[:, :LENGTH] = (shape * factor).astype(BF16).astype(F32)
        unit = pad[...]
        for bit in range(6):
            moved = pltpu.roll(unit, 2 << bit, 1)
            unit = jnp.where((moves & (1 << bit)) != 0, moved, unit)
        pad[...] = unit
        for part in range(2):
            first = pl.multiple_of(lax.rem(h + part, 2) * HALF, HALF)
            rows = pad[pl.ds(first, HALF), :]
            for b in range(SUB):
                moved = pltpu.roll(rows, 2 * b, 1) if b else rows
                at = part * HALF * SUB + b * HALF
                filt_ref[c, at : at + HALF, :] = moved.astype(BF16)
        pad[...] = jnp.zeros_like(pad)

    filters(0)
    pl.semaphore_wait(barrier, 7)
    copies = []
    for i in range(1, 8):
        copy = pltpu.make_async_remote_copy(
            src_ref=rec_ref,
            dst_ref=all_ref.at[t],
            send_sem=send.at[i],
            recv_sem=recv.at[t],
            device_id=(s, lax.rem(t + i, 8)),
            device_id_type=MESH,
        )
        copy.start()
        copies.append(copy)
    own = pltpu.make_async_copy(rec_ref, all_ref.at[t], home)
    own.start()
    filters(1)
    filters(2)
    lanes = lax.broadcasted_iota(jnp.int32, (HALF, SPREAD), 1) >> 1
    for part in range(2):
        first = pl.multiple_of(lax.rem(h + part, 2) * HALF, HALF)
        offsets = jnp.broadcast_to(mov_ref[pl.ds(first, HALF), :], (HALF, SPREAD))
        for b in range(SUB):
            at = part * HALF * SUB + b * HALF
            pick_ref[at : at + HALF, :] = jnp.where(lanes == offsets + b, 1.0, 0.0).astype(BF16)
    own.wait()
    for i in range(1, 8):
        copies[i - 1].wait_send()
        source = lax.rem(t + i, 8)
        pltpu.make_async_remote_copy(
            src_ref=rec_ref,
            dst_ref=all_ref.at[source],
            send_sem=send.at[i],
            recv_sem=recv.at[source],
            device_id=(s, source),
            device_id_type=MESH,
        ).wait_recv()


def gathered(rec, tmpl, mov):
    return pl.pallas_call(
        gather_kernel,
        out_shape=(
            jax.ShapeDtypeStruct((8, COMP, SEG), BF16),
            jax.ShapeDtypeStruct((COMP, ROWS, TAPS), BF16),
            jax.ShapeDtypeStruct((ROWS, SPREAD), BF16),
        ),
        in_specs=[pl.BlockSpec(memory_space=pltpu.VMEM)] * 3,
        out_specs=[pl.BlockSpec(memory_space=pltpu.VMEM)] * 3,
        scratch_shapes=[
            pltpu.VMEM((SHARE, TAPS), F32),
            pltpu.SemaphoreType.DMA((8,)),
            pltpu.SemaphoreType.DMA((8,)),
            pltpu.SemaphoreType.DMA,
        ],
        compiler_params=pltpu.CompilerParams(collective_id=1, has_side_effects=True, vmem_limit_bytes=32 << 20),
    )(rec, tmpl, mov)


def shifted_rows(row):
    wide = jnp.broadcast_to(row, (8, WIDE))
    low = pltpu.roll(wide, WIDE - 112, 1, stride=16, stride_axis=0)
    return jnp.concatenate([low[:, : WIDE - 128], low[:, 128:]], axis=0).astype(BF16)


def energy_scales(x):
    def ahead(v, n):
        return pltpu.roll(v, WIDE - n, 1)

    power = x * x
    two = power + ahead(power, 1)
    four = two + ahead(two, 2)
    eight = four + ahead(four, 4)
    sixteen = eight + ahead(eight, 8)
    far = sixteen + ahead(eight, 16)
    w32 = sixteen + ahead(sixteen, 16)
    w64 = w32 + ahead(w32, 32)
    w128 = w64 + ahead(w64, 64)
    w256 = w128 + ahead(w128, 128)
    w512 = w256 + ahead(w256, 256)
    energy = w512 + ahead(w64, 512) + ahead(far, 576)
    scale = lax.rsqrt(energy / LENGTH + 1e-05) / LENGTH
    high = scale.astype(BF16).astype(F32)
    low = (scale - high).astype(BF16).astype(F32)
    odd = (lax.broadcasted_iota(jnp.int32, x.shape, 1) & 1) == 1
    return jnp.where(odd, pltpu.roll(low, 1, 1), high)


def scan_kernel(all_ref, filt_ref, pick_ref, out_ref, x8, z8, base, own, part_out, part_in, sum_out, sum_in, cs, cr, ss, sr):
    s, t = lax.axis_index("sta"), lax.axis_index("tpl")
    h = lax.rem(s, 2)
    pair = lax.div(s, 2)
    sibling = (s + 1 - 2 * h, t)
    barrier = pltpu.get_barrier_semaphore()
    pl.semaphore_signal(barrier, inc=1, device_id=sibling, device_id_type=MESH)
    for j in range(8):

        @pl.when(jnp.logical_not((j == pair) & (pair == t)))
        def _():
            pl.semaphore_signal(barrier, inc=1, device_id=(2 * j + h, pair), device_id_type=MESH)

    for seg in range(8):
        block = all_ref[seg].astype(F32)
        for c in range(COMP):
            x8[c, seg : seg + 1, :SEG] = block[c : c + 1, :]
            if seg:
                x8[c, seg - 1 : seg, SEG:] = block[c : c + 1, :HALO]
    for c in range(COMP):
        x8[c, 7:8, SEG:] = jnp.zeros((1, HALO), F32)
    for c in range(COMP):
        z8[c] = energy_scales(x8[c])

    def core_copy(q):
        return pltpu.make_async_remote_copy(
            src_ref=part_out.at[q],
            dst_ref=part_in.at[q],
            send_sem=cs.at[q],
            recv_sem=cr.at[q],
            device_id=sibling,
            device_id_type=MESH,
        )

    def sum_copy(q):
        return pltpu.make_async_remote_copy(
            src_ref=sum_out.at[q],
            dst_ref=sum_in.at[pair],
            send_sem=ss.at[q],
            recv_sem=sr.at[pair],
            device_id=(2 * t + h, lax.rem(t + q, 8)),
            device_id_type=MESH,
        )

    def compute(q):
        seg = lax.rem(t + q, 8)
        for c in range(COMP):
            base[c, :, : WIDE - 128] = shifted_rows(x8[c, pl.ds(seg, 1), :])
            base[COMP + c, :, : WIDE - 128] = shifted_rows(z8[c, pl.ds(seg, 1), :])
        total = None
        for c in range(COMP):
            windows = jnp.concatenate([base[c, :, 256 * a : 256 * a + TAPS] for a in range(16)], axis=0)
            near = jnp.concatenate([base[COMP + c, :, 256 * a : 256 * a + SPREAD] for a in range(16)], axis=0)
            dims = (((1,), (1,)), ((), ()))
            number = lax.dot_general(windows, filt_ref[c], dims, preferred_element_type=F32)
            scale = lax.dot_general(near, pick_ref[...], dims, preferred_element_type=F32)
            term = number * scale
            total = term if total is None else total + term
        own[q] = total[:, :128]
        part_out[q] = total[:, 128:].astype(BF16)

    def finish(q):
        core_copy(q).wait_recv()
        both = (own[q] + part_in[q].astype(F32)).astype(BF16)
        seg = lax.rem(t + q, 8)
        mine = (pair == t) & (seg == t)

        @pl.when(mine)
        def _():
            sum_in[pair] = both

        @pl.when(jnp.logical_not(mine))
        def _():
            sum_out[q] = both
            sum_copy(q).start()

    compute(0)
    pl.semaphore_wait(barrier, 9 - (pair == t).astype(jnp.int32))
    core_copy(0).start()

    @pl.loop(1, 8)
    def _(q):
        compute(q)
        core_copy(q).start()
        finish(q - 1)

    finish(7)

    @pl.loop(0, 8)
    def _(q):
        core_copy(q).wait_send()

        @pl.when(jnp.logical_not((pair == t) & (lax.rem(t + q, 8) == t)))
        def _():
            sum_copy(q).wait_send()

    for j in range(8):

        @pl.when(jnp.logical_not((j == pair) & (pair == t)))
        def _():
            pltpu.make_async_remote_copy(
                src_ref=sum_out.at[j],
                dst_ref=sum_in.at[j],
                send_sem=ss.at[j],
                recv_sem=sr.at[j],
                device_id=(2 * t + h, t),
                device_id_type=MESH,
            ).wait_recv()

    total = sum_in[0].astype(F32)
    for j in range(1, 8):
        total = total + sum_in[j].astype(F32)
    out_ref[...] = total


def scanned(everything, filters, picks):
    return pl.pallas_call(
        scan_kernel,
        out_shape=jax.ShapeDtypeStruct((ROWS, 128), F32),
        in_specs=[pl.BlockSpec(memory_space=pltpu.VMEM)] * 3,
        out_specs=pl.BlockSpec(memory_space=pltpu.VMEM),
        scratch_shapes=[
            pltpu.VMEM((COMP, 8, WIDE), F32),
            pltpu.VMEM((COMP, 8, WIDE), F32),
            pltpu.VMEM((2 * COMP, 16, WIDE), BF16),
            pltpu.VMEM((8, ROWS, 128), F32),
            pltpu.VMEM((8, ROWS, 128), BF16),
            pltpu.VMEM((8, ROWS, 128), BF16),
            pltpu.VMEM((8, ROWS, 128), BF16),
            pltpu.VMEM((8, ROWS, 128), BF16),
            pltpu.SemaphoreType.DMA((8,)),
            pltpu.SemaphoreType.DMA((8,)),
            pltpu.SemaphoreType.DMA((8,)),
            pltpu.SemaphoreType.DMA((8,)),
        ],
        compiler_params=pltpu.CompilerParams(collective_id=2, has_side_effects=True, vmem_limit_bytes=48 << 20),
    )(everything, filters, picks)


def local(records, templates, moveouts):
    everything, filters, picks = gathered(records[0], templates[:, 0], moveouts)
    sums = scanned(everything, filters, picks)
    parts = jnp.flip(sums.reshape(ROWS // 8, 8, SUB, HALF), axis=1)
    return jnp.transpose(parts, (3, 0, 1, 2)).reshape(HALF, ROWS * SUB)


def solution(mesh):
    return jax.shard_map(
        local,
        mesh=mesh,
        in_specs=(P("sta", None, "tpl"), P("tpl", "sta", None, None), P("tpl", "sta")),
        out_specs=P("sta", "tpl"),
        check_vma=False,
    )
```

profile of v0, /device:TPU:8, one launch (start us, length us, event | category | flops | bytes accessed | tf_op | source)
XLA Modules:
  0.0 32.4 jit_solution(6342354052390049004)
XLA Ops:
  0.0 0.7 %copy.8.mov_ref = s32[32,1]{1,0:T(8,128)S(1)} copy(s32[32,1]{0,1:T(1,128)} %param.5) | data formatting | bytes 256 | tf_op args[2]
  0.7 1.0 %copy.11 = bf16[32,1,3,600]{3,2,0,1:T(4,128)(2,1)S(1)} copy(bf16[32,1,3,600]{3,0,2,1:T(8,128)(2,1)} %param.4) | data formatting | bytes 230400 | tf_op args[1]
  1.7 0.0 copy-start
  1.7 0.7 %copy-done = bf16[1,3,4096]{2,1,0:T(4,128)(2,1)S(1)} copy-done((bf16[1,3,4096]{2,1,0:T(4,128)(2,1)S(1)}, bf16[1,3,4096]{2,1,0:T(4,128)(2,1)}, u32[]{:S(2)}) %copy-start) | copy-done | bytes 24600
  2.5 7.9 %shard_map.37 = (bf16[8,3,4096]{2,1,0:T(4,128)(2,1)S(1)}, bf16[3,256,768]{2,1,0:T(8,128)(2,1)S(1)}, bf16[256,256]{1,0:T(8,128)(2,1)S(1)}) custom-call(bf16[3,4096]{1,0:T(4,128)(2,1)S(1)} %bitcast.8, bf16[32,3,600]{2,1,0:T(4,128)(2,1)S(1)} %bitcast.7, s32[32,1]{1,0:T(8,128)S(1)} %copy.8.mov_ref), custom_call_target="tpu_custom_call" | custom-call | tf_op jit(solution)/shard_map/pallas_call | solution.py:93
  10.4 20.7 %shard_map.38 = f32[256,128]{1,0:T(8,128)S(1)} custom-call(bf16[8,3,4096]{2,1,0:T(4,128)(2,1)S(1)} %get-tuple-element.8.all_ref, bf16[3,256,768]{2,1,0:T(8,128)(2,1)S(1)} %get-tuple-element.9.filt_ref, bf16[256,256]{1,0:T(8,128)(2,1)S(1)} %get-tuple-element.10.pick_ref), custom_call_target="tpu_custom_call" | custom-call | tf_op jit(solution)/shard_map/pallas_call | solution.py:257
  31.1 0.3 reshape.6
  31.4 0.1 rev.4
  31.4 1.0 %copy.9 = f32[16,2048]{1,0:T(8,128)} copy(f32[16,2048]{0,1:T(8,128)S(1)} %bitcast.9) | data formatting | bytes 262144 | tf_op jit(solution)/shard_map/reshape | solution.py:284
Async XLA Ops:
  1.7 0.8 %copy-start = (bf16[1,3,4096]{2,1,0:T(4,128)(2,1)S(1)}, bf16[1,3,4096]{2,1,0:T(4,128)(2,1)}, u32[]{:S(2)}) copy-start(bf16[1,3,4096]{2,1,0:T(4,128)(2,1)} %param.3) | copy-start | bytes 73732
where the time goes:
time: 33 us; the launch traced here: 32.4 us
  Pallas kernels  28.5 us (86%)
  local copies, waits for them, and re-layouts  3.82 us (12%)
    pallas_call x1, Pallas kernels, scanned(): pl.pallas_call(scan_kernel, out_shape=jax.ShapeDtypeStruct((ROWS, 128), F...  20.7 us
    pallas_call x1, Pallas kernels, gathered(): pl.pallas_call(gather_kernel, out_shape=(jax.ShapeDtypeStruct((8, COMP, S...  7.89 us
    unnamed x4, local copies, waits for them, and re-layouts  2.47 us
    reshape x1, local copies, waits for them, and re-layouts, local(): return jnp.transpose(parts, (3, 0, 1, 2)).reshape(HALF, ROWS * SUB)  0.96 us

commit v1 on v0

--- a/solution.py
+++ b/solution.py
@@ -22,18 +22,29 @@
 ROWS = 256
 
 
-def gather_kernel(rec_ref, tmpl_ref, mov_ref, all_ref, filt_ref, pick_ref, pad, send, recv, home):
+def gather_kernel(rec_hbm, tmpl_hbm, mov_hbm, all_ref, filt_ref, pick_ref, tmpl_ref, mov_row, mov_ref, pad, send, recv, home):
     s, t = lax.axis_index("sta"), lax.axis_index("tpl")
     h = lax.rem(s, 2)
     barrier = pltpu.get_barrier_semaphore()
     for i in range(1, 8):
         pl.semaphore_signal(barrier, inc=1, device_id=(s, lax.rem(t + i, 8)), device_id_type=MESH)
 
+    own = pltpu.make_async_copy(rec_hbm, all_ref.at[t], home.at[0])
+    own.start()
+    tmpl = pltpu.make_async_copy(tmpl_hbm, tmpl_ref, home.at[1])
+    tmpl.start()
+    shift = pltpu.make_async_copy(mov_hbm, mov_row, home.at[2])
+    shift.start()
     pad[...] = jnp.zeros_like(pad)
+    shift.wait()
+    square = (SHARE, SHARE)
+    diagonal = lax.broadcasted_iota(jnp.int32, square, 0) == lax.broadcasted_iota(jnp.int32, square, 1)
+    mov_ref[...] = jnp.sum(jnp.where(diagonal, jnp.broadcast_to(mov_row[...], square), 0), axis=1, keepdims=True)
     moves = jnp.broadcast_to(mov_ref[...], (SHARE, TAPS))
+    tmpl.wait()
 
     def filters(c):
-        shape = tmpl_ref[:, c, :].astype(F32)
+        shape = tmpl_ref[c].astype(F32)
         factor = lax.rsqrt(jnp.sum(shape * shape, axis=1, keepdims=True) / LENGTH + 1e-05)
         pad[:, :LENGTH] = (shape * factor).astype(BF16).astype(F32)
         unit = pad[...]
@@ -51,11 +62,12 @@
         pad[...] = jnp.zeros_like(pad)
 
     filters(0)
+    own.wait()
     pl.semaphore_wait(barrier, 7)
     copies = []
     for i in range(1, 8):
         copy = pltpu.make_async_remote_copy(
-            src_ref=rec_ref,
+            src_ref=all_ref.at[t],
             dst_ref=all_ref.at[t],
             send_sem=send.at[i],
             recv_sem=recv.at[t],
@@ -64,8 +76,6 @@
         )
         copy.start()
         copies.append(copy)
-    own = pltpu.make_async_copy(rec_ref, all_ref.at[t], home)
-    own.start()
     filters(1)
     filters(2)
     lanes = lax.broadcasted_iota(jnp.int32, (HALF, SPREAD), 1) >> 1
@@ -75,12 +85,11 @@
         for b in range(SUB):
             at = part * HALF * SUB + b * HALF
             pick_ref[at : at + HALF, :] = jnp.where(lanes == offsets + b, 1.0, 0.0).astype(BF16)
-    own.wait()
     for i in range(1, 8):
         copies[i - 1].wait_send()
         source = lax.rem(t + i, 8)
         pltpu.make_async_remote_copy(
-            src_ref=rec_ref,
+            src_ref=all_ref.at[t],
             dst_ref=all_ref.at[source],
             send_sem=send.at[i],
             recv_sem=recv.at[source],
@@ -97,13 +106,16 @@
             jax.ShapeDtypeStruct((COMP, ROWS, TAPS), BF16),
             jax.ShapeDtypeStruct((ROWS, SPREAD), BF16),
         ),
-        in_specs=[pl.BlockSpec(memory_space=pltpu.VMEM)] * 3,
+        in_specs=[pl.BlockSpec(memory_space=pltpu.HBM)] * 3,
         out_specs=[pl.BlockSpec(memory_space=pltpu.VMEM)] * 3,
         scratch_shapes=[
+            pltpu.VMEM((COMP, SHARE, LENGTH), BF16),
+            pltpu.VMEM((1, SHARE), jnp.int32),
+            pltpu.VMEM((SHARE, 1), jnp.int32),
             pltpu.VMEM((SHARE, TAPS), F32),
             pltpu.SemaphoreType.DMA((8,)),
             pltpu.SemaphoreType.DMA((8,)),
-            pltpu.SemaphoreType.DMA,
+            pltpu.SemaphoreType.DMA((3,)),
         ],
         compiler_params=pltpu.CompilerParams(collective_id=1, has_side_effects=True, vmem_limit_bytes=32 << 20),
     )(rec, tmpl, mov)
@@ -178,12 +190,12 @@
             dst_ref=sum_in.at[pair],
             send_sem=ss.at[q],
             recv_sem=sr.at[pair],
-            device_id=(2 * t + h, lax.rem(t + q, 8)),
+            device_id=(2 * t + h, lax.rem(pair + q, 8)),
             device_id_type=MESH,
         )
 
     def compute(q):
-        seg = lax.rem(t + q, 8)
+        seg = lax.rem(pair + q, 8)
         for c in range(COMP):
             base[c, :, : WIDE - 128] = shifted_rows(x8[c, pl.ds(seg, 1), :])
             base[COMP + c, :, : WIDE - 128] = shifted_rows(z8[c, pl.ds(seg, 1), :])
@@ -202,7 +214,7 @@
     def finish(q):
         core_copy(q).wait_recv()
         both = (own[q] + part_in[q].astype(F32)).astype(BF16)
-        seg = lax.rem(t + q, 8)
+        seg = lax.rem(pair + q, 8)
         mine = (pair == t) & (seg == t)
 
         @pl.when(mine)
@@ -230,7 +242,7 @@
     def _(q):
         core_copy(q).wait_send()
 
-        @pl.when(jnp.logical_not((pair == t) & (lax.rem(t + q, 8) == t)))
+        @pl.when(jnp.logical_not((pair == t) & (lax.rem(pair + q, 8) == t)))
         def _():
             sum_copy(q).wait_send()
 
@@ -278,7 +290,8 @@
 
 
 def local(records, templates, moveouts):
-    everything, filters, picks = gathered(records[0], templates[:, 0], moveouts)
+    operands = (records[0], jnp.transpose(templates[:, 0], (1, 0, 2)), jnp.transpose(moveouts))
+    everything, filters, picks = gathered(*[pltpu.with_memory_space_constraint(v, pltpu.HBM) for v in operands])
     sums = scanned(everything, filters, picks)
     parts = jnp.flip(sums.reshape(ROWS // 8, 8, SUB, HALF), axis=1)
     return jnp.transpose(parts, (3, 0, 1, 2)).reshape(HALF, ROWS * SUB)

time: 33 us -> 30.1 us (0.912); the launches traced: 32.4 us -> 30 us
  local copies, waits for them, and re-layouts: 3.82 us -> 1.34 us
    unnamed x4 -> x0, local copies, waits for them, and re-layouts: 2.47 us -> none
    pallas_call x1, Pallas kernels: 7.89 us -> 8.46 us  [gathered(): pl.pallas_call(gather_kernel, out_shape=(jax.ShapeDtypeStruct((8, COMP, S...]
    pallas_call x1, Pallas kernels: 20.7 us -> 20.1 us  [scanned(): pl.pallas_call(scan_kernel, out_shape=jax.ShapeDtypeStruct((ROWS, 128), F...]
where the time goes in v1:
time: 30.1 us; the launch traced here: 30 us
  Pallas kernels  28.6 us (95%)
  local copies, waits for them, and re-layouts  1.34 us (4%)
    pallas_call x1, Pallas kernels, scanned(): pl.pallas_call(scan_kernel, out_shape=jax.ShapeDtypeStruct((ROWS, 128), F...  20.1 us
    pallas_call x1, Pallas kernels, gathered(): pl.pallas_call(gather_kernel, out_shape=(jax.ShapeDtypeStruct((8, COMP, S...  8.46 us
    reshape x1, local copies, waits for them, and re-layouts, local(): return jnp.transpose(parts, (3, 0, 1, 2)).reshape(HALF, ROWS * SUB)  0.96 us

profile of v1, /device:TPU:8, one launch (start us, length us, event | category | flops | bytes accessed | tf_op | source)
XLA Modules:
  0.0 30.0 jit_solution(9425334627828182305)
XLA Ops:
  0.0 8.5 %shard_map.37 = (bf16[8,3,4096]{2,1,0:T(4,128)(2,1)S(1)}, bf16[3,256,768]{2,1,0:T(8,128)(2,1)S(1)}, bf16[256,256]{1,0:T(8,128)(2,1)S(1)}) custom-call(bf16[3,4096]{1,0:T(4,128)(2,1)} %bitcast.10, bf16[3,32,600]{2,1,0:T(8,128)(2,1)} %bitcast.9, s32[1,32]{1,0:T(1,128)} %bitcast.11), custom_call_target="tpu_custom_call" | custom-call | tf_op jit(solution)/shard_map/pallas_call | solution.py:102
  8.5 20.1 %shard_map.38 = f32[256,128]{1,0:T(8,128)S(1)} custom-call(bf16[8,3,4096]{2,1,0:T(4,128)(2,1)S(1)} %get-tuple-element.8.all_ref, bf16[3,256,768]{2,1,0:T(8,128)(2,1)S(1)} %get-tuple-element.9.filt_ref, bf16[256,256]{1,0:T(8,128)(2,1)S(1)} %get-tuple-element.10.pick_ref), custom_call_target="tpu_custom_call" | custom-call | tf_op jit(solution)/shard_map/pallas_call | solution.py:269
  28.6 0.3 %reshape.6 = f32[32,8,8,16]{3,2,1,0:T(8,128)S(1)} reshape(f32[256,128]{1,0:T(8,128)S(1)} %shard_map.38) | data formatting | bytes 262144 | tf_op jit(solution)/shard_map/reshape | solution.py:296
  28.9 0.1 rev.4
  29.0 1.0 %copy.5 = f32[16,2048]{1,0:T(8,128)} copy(f32[16,2048]{0,1:T(8,128)S(1)} %bitcast.8) | data formatting | bytes 262144 | tf_op jit(solution)/shard_map/reshape | solution.py:297

commit v2 on v1

--- a/solution.py
+++ b/solution.py
@@ -20,14 +20,16 @@
 HALF = 16
 SUB = 8
 ROWS = 256
+ORDER = (6, 7, 5, 2, 4, 3, 1)
+NEAR = (6, 7, 5, 2, 4, 3, 1, 0)
 
 
 def gather_kernel(rec_hbm, tmpl_hbm, mov_hbm, all_ref, filt_ref, pick_ref, tmpl_ref, mov_row, mov_ref, pad, send, recv, home):
     s, t = lax.axis_index("sta"), lax.axis_index("tpl")
     h = lax.rem(s, 2)
     barrier = pltpu.get_barrier_semaphore()
-    for i in range(1, 8):
-        pl.semaphore_signal(barrier, inc=1, device_id=(s, lax.rem(t + i, 8)), device_id_type=MESH)
+    for i in ORDER:
+        pl.semaphore_signal(barrier, inc=1, device_id=(s, t ^ i), device_id_type=MESH)
 
     own = pltpu.make_async_copy(rec_hbm, all_ref.at[t], home.at[0])
     own.start()
@@ -65,13 +67,13 @@
     own.wait()
     pl.semaphore_wait(barrier, 7)
     copies = []
-    for i in range(1, 8):
+    for i in ORDER:
         copy = pltpu.make_async_remote_copy(
             src_ref=all_ref.at[t],
             dst_ref=all_ref.at[t],
             send_sem=send.at[i],
             recv_sem=recv.at[t],
-            device_id=(s, lax.rem(t + i, 8)),
+            device_id=(s, t ^ i),
             device_id_type=MESH,
         )
         copy.start()
@@ -85,9 +87,10 @@
         for b in range(SUB):
             at = part * HALF * SUB + b * HALF
             pick_ref[at : at + HALF, :] = jnp.where(lanes == offsets + b, 1.0, 0.0).astype(BF16)
-    for i in range(1, 8):
-        copies[i - 1].wait_send()
-        source = lax.rem(t + i, 8)
+    for copy in copies:
+        copy.wait_send()
+    for i in ORDER:
+        source = t ^ i
         pltpu.make_async_remote_copy(
             src_ref=all_ref.at[t],
             dst_ref=all_ref.at[source],
@@ -157,7 +160,8 @@
     sibling = (s + 1 - 2 * h, t)
     barrier = pltpu.get_barrier_semaphore()
     pl.semaphore_signal(barrier, inc=1, device_id=sibling, device_id_type=MESH)
-    for j in range(8):
+    for i in NEAR:
+        j = pair ^ i
 
         @pl.when(jnp.logical_not((j == pair) & (pair == t)))
         def _():

time: 30.1 us -> 29.8 us (0.990)
  no operation moved by 1% of the time
where the time goes in v2:
time: 29.8 us; the launch traced here: 29.7 us
  Pallas kernels  28.3 us (95%)
  local copies, waits for them, and re-layouts  1.34 us (4%)
    pallas_call x1, Pallas kernels, scanned(): pl.pallas_call(scan_kernel, out_shape=jax.ShapeDtypeStruct((ROWS, 128), F...  20.1 us
    pallas_call x1, Pallas kernels, gathered(): pl.pallas_call(gather_kernel, out_shape=(jax.ShapeDtypeStruct((8, COMP, S...  8.18 us
    reshape x1, local copies, waits for them, and re-layouts, local(): return jnp.transpose(parts, (3, 0, 1, 2)).reshape(HALF, ROWS * SUB)  0.96 us

profile of v2, /device:TPU:8, one launch (start us, length us, event | category | flops | bytes accessed | tf_op | source)
XLA Modules:
  0.0 29.7 jit_solution(8763227237387679203)
XLA Ops:
  0.0 8.2 %shard_map.37 = (bf16[8,3,4096]{2,1,0:T(4,128)(2,1)S(1)}, bf16[3,256,768]{2,1,0:T(8,128)(2,1)S(1)}, bf16[256,256]{1,0:T(8,128)(2,1)S(1)}) custom-call(bf16[3,4096]{1,0:T(4,128)(2,1)} %bitcast.10, bf16[3,32,600]{2,1,0:T(8,128)(2,1)} %bitcast.9, s32[1,32]{1,0:T(1,128)} %bitcast.11), custom_call_target="tpu_custom_call" | custom-call | tf_op jit(solution)/shard_map/pallas_call | solution.py:105
  8.2 20.1 %shard_map.38 = f32[256,128]{1,0:T(8,128)S(1)} custom-call(bf16[8,3,4096]{2,1,0:T(4,128)(2,1)S(1)} %get-tuple-element.8.all_ref, bf16[3,256,768]{2,1,0:T(8,128)(2,1)S(1)} %get-tuple-element.9.filt_ref, bf16[256,256]{1,0:T(8,128)(2,1)S(1)} %get-tuple-element.10.pick_ref), custom_call_target="tpu_custom_call" | custom-call | tf_op jit(solution)/shard_map/pallas_call | solution.py:273
  28.3 0.3 %reshape.6 = f32[32,8,8,16]{3,2,1,0:T(8,128)S(1)} reshape(f32[256,128]{1,0:T(8,128)S(1)} %shard_map.38) | data formatting | bytes 262144 | tf_op jit(solution)/shard_map/reshape | solution.py:300
  28.7 0.1 rev.4
  28.7 1.0 %copy.5 = f32[16,2048]{1,0:T(8,128)} copy(f32[16,2048]{0,1:T(8,128)S(1)} %bitcast.8) | data formatting | bytes 262144 | tf_op jit(solution)/shard_map/reshape | solution.py:301

commit v3 on v2

--- a/solution.py
+++ b/solution.py
@@ -234,12 +234,16 @@
     pl.semaphore_wait(barrier, 9 - (pair == t).astype(jnp.int32))
     core_copy(0).start()
 
-    @pl.loop(1, 8)
+    compute(1)
+    core_copy(1).start()
+
+    @pl.loop(2, 8)
     def _(q):
         compute(q)
         core_copy(q).start()
-        finish(q - 1)
-
+        finish(q - 2)
+
+    finish(6)
     finish(7)
 
     @pl.loop(0, 8)

time: 29.8 us -> 29.1 us (0.977)
  Pallas kernels: 28.3 us -> 27.6 us
    pallas_call x1, Pallas kernels: 20.1 us -> 19.4 us  [scanned(): pl.pallas_call(scan_kernel, out_shape=jax.ShapeDtypeStruct((ROWS, 128), F...]
where the time goes in v3:
time: 29.1 us; the launch traced here: 28.9 us
  Pallas kernels  27.6 us (95%)
  local copies, waits for them, and re-layouts  1.34 us (5%)
    pallas_call x1, Pallas kernels, scanned(): pl.pallas_call(scan_kernel, out_shape=jax.ShapeDtypeStruct((ROWS, 128), F...  19.4 us
    pallas_call x1, Pallas kernels, gathered(): pl.pallas_call(gather_kernel, out_shape=(jax.ShapeDtypeStruct((8, COMP, S...  8.18 us
    reshape x1, local copies, waits for them, and re-layouts, local(): return jnp.transpose(parts, (3, 0, 1, 2)).reshape(HALF, ROWS * SUB)  0.96 us

profile of v3, /device:TPU:8, one launch (start us, length us, event | category | flops | bytes accessed | tf_op | source)
XLA Modules:
  0.0 28.9 jit_solution(6278301271964028135)
XLA Ops:
  0.0 8.2 %shard_map.37 = (bf16[8,3,4096]{2,1,0:T(4,128)(2,1)S(1)}, bf16[3,256,768]{2,1,0:T(8,128)(2,1)S(1)}, bf16[256,256]{1,0:T(8,128)(2,1)S(1)}) custom-call(bf16[3,4096]{1,0:T(4,128)(2,1)} %bitcast.10, bf16[3,32,600]{2,1,0:T(8,128)(2,1)} %bitcast.9, s32[1,32]{1,0:T(1,128)} %bitcast.11), custom_call_target="tpu_custom_call" | custom-call | tf_op jit(solution)/shard_map/pallas_call | solution.py:105
  8.2 19.4 %shard_map.38 = f32[256,128]{1,0:T(8,128)S(1)} custom-call(bf16[8,3,4096]{2,1,0:T(4,128)(2,1)S(1)} %get-tuple-element.8.all_ref, bf16[3,256,768]{2,1,0:T(8,128)(2,1)S(1)} %get-tuple-element.9.filt_ref, bf16[256,256]{1,0:T(8,128)(2,1)S(1)} %get-tuple-element.10.pick_ref), custom_call_target="tpu_custom_call" | custom-call | tf_op jit(solution)/shard_map/pallas_call | solution.py:277
  27.6 0.3 %reshape.6 = f32[32,8,8,16]{3,2,1,0:T(8,128)S(1)} reshape(f32[256,128]{1,0:T(8,128)S(1)} %shard_map.38) | data formatting | bytes 262144 | tf_op jit(solution)/shard_map/reshape | solution.py:304
  27.9 0.1 rev.4
  28.0 1.0 %copy.5 = f32[16,2048]{1,0:T(8,128)} copy(f32[16,2048]{0,1:T(8,128)S(1)} %bitcast.8) | data formatting | bytes 262144 | tf_op jit(solution)/shard_map/reshape | solution.py:305

commit v4 on v3

--- a/solution.py
+++ b/solution.py
@@ -43,7 +43,6 @@
     diagonal = lax.broadcasted_iota(jnp.int32, square, 0) == lax.broadcasted_iota(jnp.int32, square, 1)
     mov_ref[...] = jnp.sum(jnp.where(diagonal, jnp.broadcast_to(mov_row[...], square), 0), axis=1, keepdims=True)
     moves = jnp.broadcast_to(mov_ref[...], (SHARE, TAPS))
-    tmpl.wait()
 
     def filters(c):
         shape = tmpl_ref[c].astype(F32)
@@ -63,7 +62,6 @@
                 filt_ref[c, at : at + HALF, :] = moved.astype(BF16)
         pad[...] = jnp.zeros_like(pad)
 
-    filters(0)
     own.wait()
     pl.semaphore_wait(barrier, 7)
     copies = []
@@ -78,8 +76,9 @@
         )
         copy.start()
         copies.append(copy)
-    filters(1)
-    filters(2)
+    tmpl.wait()
+    for c in range(COMP):
+        filters(c)
     lanes = lax.broadcasted_iota(jnp.int32, (HALF, SPREAD), 1) >> 1
     for part in range(2):
         first = pl.multiple_of(lax.rem(h + part, 2) * HALF, HALF)

time: 29.1 us -> 29 us (level)
  no operation moved by 1% of the time
where the time goes in v4:
time: 29 us; the launch traced here: 28.9 us
  Pallas kernels  27.6 us (95%)
  local copies, waits for them, and re-layouts  1.34 us (5%)
    pallas_call x1, Pallas kernels, scanned(): pl.pallas_call(scan_kernel, out_shape=jax.ShapeDtypeStruct((ROWS, 128), F...  19.7 us
    pallas_call x1, Pallas kernels, gathered(): pl.pallas_call(gather_kernel, out_shape=(jax.ShapeDtypeStruct((8, COMP, S...  7.9 us
    reshape x1, local copies, waits for them, and re-layouts, local(): return jnp.transpose(parts, (3, 0, 1, 2)).reshape(HALF, ROWS * SUB)  0.96 us

profile of v4, /device:TPU:8, one launch (start us, length us, event | category | flops | bytes accessed | tf_op | source)
XLA Modules:
  0.0 28.9 jit_solution(2480061553809461300)
XLA Ops:
  0.0 7.9 %shard_map.37 = (bf16[8,3,4096]{2,1,0:T(4,128)(2,1)S(1)}, bf16[3,256,768]{2,1,0:T(8,128)(2,1)S(1)}, bf16[256,256]{1,0:T(8,128)(2,1)S(1)}) custom-call(bf16[3,4096]{1,0:T(4,128)(2,1)} %bitcast.10, bf16[3,32,600]{2,1,0:T(8,128)(2,1)} %bitcast.9, s32[1,32]{1,0:T(1,128)} %bitcast.11), custom_call_target="tpu_custom_call" | custom-call | tf_op jit(solution)/shard_map/pallas_call | solution.py:104
  7.9 19.7 %shard_map.38 = f32[256,128]{1,0:T(8,128)S(1)} custom-call(bf16[8,3,4096]{2,1,0:T(4,128)(2,1)S(1)} %get-tuple-element.8.all_ref, bf16[3,256,768]{2,1,0:T(8,128)(2,1)S(1)} %get-tuple-element.9.filt_ref, bf16[256,256]{1,0:T(8,128)(2,1)S(1)} %get-tuple-element.10.pick_ref), custom_call_target="tpu_custom_call" | custom-call | tf_op jit(solution)/shard_map/pallas_call | solution.py:276
  27.6 0.3 %reshape.6 = f32[32,8,8,16]{3,2,1,0:T(8,128)S(1)} reshape(f32[256,128]{1,0:T(8,128)S(1)} %shard_map.38) | data formatting | bytes 262144 | tf_op jit(solution)/shard_map/reshape | solution.py:303
  27.9 0.1 rev.4
  28.0 1.0 %copy.5 = f32[16,2048]{1,0:T(8,128)} copy(f32[16,2048]{0,1:T(8,128)S(1)} %bitcast.8) | data formatting | bytes 262144 | tf_op jit(solution)/shard_map/reshape | solution.py:304

commit v5 on v4

--- a/solution.py
+++ b/solution.py
@@ -157,6 +157,11 @@
     h = lax.rem(s, 2)
     pair = lax.div(s, 2)
     sibling = (s + 1 - 2 * h, t)
+    y_hi = lax.div(pair, 4)
+
+    def chunk(q):
+        return 4 * lax.rem(1 - y_hi + lax.div(q, 4), 2) + lax.rem(pair + q, 4)
+
     barrier = pltpu.get_barrier_semaphore()
     pl.semaphore_signal(barrier, inc=1, device_id=sibling, device_id_type=MESH)
     for i in NEAR:
@@ -193,12 +198,12 @@
             dst_ref=sum_in.at[pair],
             send_sem=ss.at[q],
             recv_sem=sr.at[pair],
-            device_id=(2 * t + h, lax.rem(pair + q, 8)),
+            device_id=(2 * t + h, chunk(q)),
             device_id_type=MESH,
         )
 
     def compute(q):
-        seg = lax.rem(pair + q, 8)
+        seg = chunk(q)
         for c in range(COMP):
             base[c, :, : WIDE - 128] = shifted_rows(x8[c, pl.ds(seg, 1), :])
             base[COMP + c, :, : WIDE - 128] = shifted_rows(z8[c, pl.ds(seg, 1), :])
@@ -217,7 +222,7 @@
     def finish(q):
         core_copy(q).wait_recv()
         both = (own[q] + part_in[q].astype(F32)).astype(BF16)
-        seg = lax.rem(pair + q, 8)
+        seg = chunk(q)
         mine = (pair == t) & (seg == t)
 
         @pl.when(mine)
@@ -249,7 +254,7 @@
     def _(q):
         core_copy(q).wait_send()
 
-        @pl.when(jnp.logical_not((pair == t) & (lax.rem(pair + q, 8) == t)))
+        @pl.when(jnp.logical_not((pair == t) & (chunk(q) == t)))
         def _():
             sum_copy(q).wait_send()
 

time: 29 us -> 29.1 us (level)
  no operation moved by 1% of the time
where the time goes in v5:
time: 29.1 us; the launch traced here: 29 us
  Pallas kernels  27.6 us (95%)
  local copies, waits for them, and re-layouts  1.34 us (5%)
    pallas_call x1, Pallas kernels, scanned(): pl.pallas_call(scan_kernel, out_shape=jax.ShapeDtypeStruct((ROWS, 128), F...  19.7 us
    pallas_call x1, Pallas kernels, gathered(): pl.pallas_call(gather_kernel, out_shape=(jax.ShapeDtypeStruct((8, COMP, S...  7.9 us
    reshape x1, local copies, waits for them, and re-layouts, local(): return jnp.transpose(parts, (3, 0, 1, 2)).reshape(HALF, ROWS * SUB)  0.96 us

profile of v5, /device:TPU:8, one launch (start us, length us, event | category | flops | bytes accessed | tf_op | source)
XLA Modules:
  0.0 29.0 jit_solution(5927222509974685425)
XLA Ops:
  0.0 7.9 %shard_map.37 = (bf16[8,3,4096]{2,1,0:T(4,128)(2,1)S(1)}, bf16[3,256,768]{2,1,0:T(8,128)(2,1)S(1)}, bf16[256,256]{1,0:T(8,128)(2,1)S(1)}) custom-call(bf16[3,4096]{1,0:T(4,128)(2,1)} %bitcast.10, bf16[3,32,600]{2,1,0:T(8,128)(2,1)} %bitcast.9, s32[1,32]{1,0:T(1,128)} %bitcast.11), custom_call_target="tpu_custom_call" | custom-call | tf_op jit(solution)/shard_map/pallas_call | solution.py:104
  7.9 19.7 %shard_map.38 = f32[256,128]{1,0:T(8,128)S(1)} custom-call(bf16[8,3,4096]{2,1,0:T(4,128)(2,1)S(1)} %get-tuple-element.8.all_ref, bf16[3,256,768]{2,1,0:T(8,128)(2,1)S(1)} %get-tuple-element.9.filt_ref, bf16[256,256]{1,0:T(8,128)(2,1)S(1)} %get-tuple-element.10.pick_ref), custom_call_target="tpu_custom_call" | custom-call | tf_op jit(solution)/shard_map/pallas_call | solution.py:281
  27.6 0.3 %reshape.6 = f32[32,8,8,16]{3,2,1,0:T(8,128)S(1)} reshape(f32[256,128]{1,0:T(8,128)S(1)} %shard_map.38) | data formatting | bytes 262144 | tf_op jit(solution)/shard_map/reshape | solution.py:308
  27.9 0.1 rev.4
  28.0 1.0 %copy.5 = f32[16,2048]{1,0:T(8,128)} copy(f32[16,2048]{0,1:T(8,128)S(1)} %bitcast.8) | data formatting | bytes 262144 | tf_op jit(solution)/shard_map/reshape | solution.py:309
